TPU v7x, 256 devices: a whole 4x4x8 slice. The times are simulated.
256 devices in a mesh: enc: 16 (over z_hi, x), dec: 8 (over y, core), grp: 2 (over z_lo).
Axes of the slice: x: 4, y: 4, z: 8 (z_hi: 4, z_lo: 2; z = z_hi * 2 + z_lo), core: 2. Of those that a mesh axis runs over, the one named last changes fastest.
Arguments:
- images: bfloat16 [256, 4, 32, 1280], P(('enc', 'dec', 'grp')), may hold values from -6 to 6
- ln_gain: float32 [1280], replicated, may hold values from 0.1 to 1.9
- ln_bias: float32 [1280], replicated, may hold values from -3 to 3
- fc1_weight: bfloat16 [5120, 1280], P('enc'), may hold values from -0.15625 to 0.15625
- fc1_bias: float32 [5120], P('enc'), may hold values from -3 to 3
- fc2_weight: bfloat16 [5120, 1280], P('enc'), may hold values from -0.078125 to 0.078125
- fc2_bias: float32 [1280], replicated, may hold values from -3 to 3
- key_weight: bfloat16 [1280, 512], replicated, may hold values from -0.15625 to 0.15625
- value_weight: bfloat16 [1280, 512], replicated, may hold values from -0.15625 to 0.15625
- text: bfloat16 [64, 128, 8192], P(('enc', 'grp')), may hold values from -6 to 6
- query_weight: bfloat16 [8192, 4096], P('enc', 'dec'), may hold values from -0.0625 to 0.0625
- tiles: int32 [16, 8, 2], replicated, may hold values from 1 to 4, as said below
- links: int32 [64, 8], P(('enc', 'grp')), may hold values from 0 to 1, as said below
- lengths: int32 [64], P(('enc', 'grp')), may hold values from 1 to 128
- state_grads: bfloat16 [256, 4, 32, 1280], P(('enc', 'dec', 'grp')), may hold values from -0.125 to 0.125
Outputs:
- context: bfloat16 [64, 128, 4096], P(('enc', 'grp'), None, 'dec')
- fc1_grad: float32 [5120, 1280], P(('enc', 'dec', 'grp'))
- fc2_grad: float32 [5120, 1280], P(('enc', 'dec', 'grp'))
Inputs may be any that keep to these rules, and one draw needn't show every extreme that they name: The 16 images that share their last two indices have 40 tiles together, and one of them has 4. `links`: every text is linked to at least one image.
All inputs are finite; a program needn't handle non-finite values.
Results may differ from a plain program's by a relative error of at most 0.017.
Values may be sent and summed in bfloat16 or wider, within the bound.
No kernel may reach another device: no remote copies, remote signals or barrier semaphores. Data moves between devices by JAX's collectives and lax.ppermute only.
A program may use at most 128 MiB of HBM per device.

v0:
```python
import jax
import jax.numpy as jnp
from jax import lax
from jax.experimental import pallas as pl
from jax.experimental.pallas import tpu as pltpu
from jax.sharding import Mesh
from jax.sharding import PartitionSpec as P

HEADS = 32
KV_HEADS = 4
HD = 128
EPSILON = 1e-06
F32 = jnp.float32
BF16 = jnp.bfloat16
NT = (((1,), (1,)), ((), ()))
NN = (((1,), (0,)), ((), ()))
NX, NZ, NY, NC, NG = 4, 4, 4, 2, 2


def dot(a, b, dims):
    return lax.dot_general(a, b, dims, preferred_element_type=F32)


def local(body, outs, *args, scalars=0, raw=0, scratch=(), flops=0, limit=40, after=()):
    taken = len(args)

    def ordered(*refs):
        body(*refs[:taken], *refs[taken + len(after) :])

    moved = sum(a.size * a.dtype.itemsize for a in args)
    moved += sum(o.size * o.dtype.itemsize for o in outs)
    in_specs = [pl.BlockSpec(memory_space=pltpu.SMEM)] * scalars
    in_specs += [pl.BlockSpec(memory_space=pltpu.VMEM)] * (len(args) - scalars - raw)
    in_specs += [pl.BlockSpec(memory_space=pl.ANY)] * (raw + len(after))
    return pl.pallas_call(
        ordered,
        out_shape=tuple(outs),
        in_specs=in_specs,
        out_specs=tuple(pl.BlockSpec(memory_space=pltpu.VMEM) for _ in outs),
        scratch_shapes=scratch,
        compiler_params=pltpu.CompilerParams(vmem_limit_bytes=limit << 20),
        cost_estimate=pl.CostEstimate(flops=flops, transcendentals=0, bytes_accessed=moved),
    )(*args, *after)


def sds(shape, dtype):
    return jax.ShapeDtypeStruct(shape, dtype)


def pull(array, axis, step):
    n = lax.axis_size(axis)
    return lax.ppermute(array, axis, [((i + step) % n, i) for i in range(n)])


def push(array, axis, step):
    n = lax.axis_size(axis)
    return lax.ppermute(array, axis, [(i, (i + step) % n) for i in range(n)])


def prepare(place, x, gain, shift, grads, b1, w1, w2, both, piece, terms, sem):
    width = x.shape[1]
    share = piece.shape[0] // 2
    start = pl.multiple_of(place[0], 8)
    copies = [
        pltpu.make_async_copy(
            w.at[pl.ds(start, share), :], piece.at[pl.ds(m * share, share), pl.ds(0, width)], sem.at[m]
        )
        for m, w in enumerate((w1, w2))
    ]
    for copy in copies:
        copy.start()
    tile = x.shape[0]
    values = x[...].astype(F32)
    middle = jnp.mean(values, axis=-1, keepdims=True)
    centered = values - middle
    spread = jnp.mean(centered * centered, axis=-1, keepdims=True)
    normed = (centered * lax.rsqrt(spread + EPSILON) * gain[...] + shift[...]).astype(BF16)
    given = grads[...]
    for j in range(NX):
        both[j, :tile] = normed
        both[j, tile:] = given
    count = b1.shape[1]
    row = lax.broadcasted_iota(jnp.int32, (count, count), 0)
    lane = lax.broadcasted_iota(jnp.int32, (count, count), 1)
    column = jnp.sum(jnp.where(row == lane, b1[...], 0.0), axis=1, keepdims=True)
    first = column.astype(BF16).astype(F32)
    second = (column - first).astype(BF16).astype(F32)
    third = column - first - second
    lane = lax.broadcasted_iota(jnp.int32, terms.shape, 1)
    terms[...] = jnp.where(
        lane == 0, first, jnp.where(lane == 1, second, jnp.where(lane == 2, third, 0.0))
    ).astype(BF16)
    piece[:share, width:] = terms[pl.ds(start, share), :]
    piece[share:, width:] = jnp.zeros((share, piece.shape[1] - width), BF16)
    for copy in copies:
        copy.wait()


def join(a, b, c, out):
    n = a.shape[0]
    out[:n, :] = a[...]
    out[n : 2 * n, :] = b[...]
    out[2 * n :, :] = c[...]


def forward(place, w1, w2, terms, *refs):
    pieces, both = refs[:8], refs[8]
    hidden, slope, second, send, first, bias, whole = refs[9:]
    share = pieces[0].shape[0] // 6
    width = w1.shape[1]
    tile = both.shape[1] // 2
    for j in range(NX):
        whole[j * tile : (j + 1) * tile, :] = both[j, :tile]
    for jc in range(NC):
        for jy in range(NY):
            at = (jc * NY + jy) * NZ * share
            peer = ((place[0] + jy) % NY) * NC + (place[1] + jc) % NC
            start = pl.multiple_of(peer * share, 8)
            first[at : at + share, :] = w1[pl.ds(start, share), :]
            second[at : at + share, :] = w2[pl.ds(start, share), :]
            bias[at : at + share, :] = terms[pl.ds(start, share), :]
            piece = pieces[jc * NY + jy]
            for jz in range(1, NZ):
                to, own = at + jz * share, (jz - 1) * 2 * share
                first[to : to + share, :] = piece[own : own + share, :width]
                second[to : to + share, :] = piece[own + share : own + 2 * share, :width]
                bias[to : to + share, :] = piece[own : own + share, width:]
    count = first.shape[0]
    step = 256
    for at in range(0, count, step):
        pre = dot(first[at : at + step, :], whole[...], NT)
        pre = pre + jnp.sum(bias[at : at + step, :].astype(F32), axis=1, keepdims=True)
        phi = 0.5 * (1.0 + lax.erf(pre * 0.7071067811865476))
        hidden[at : at + step, :] = (pre * phi).astype(BF16)
        slope[at : at + step, :] = phi + pre * jnp.exp(-0.5 * pre * pre) * 0.3989422804014327
    turned = jnp.swapaxes(hidden[...], 0, 1)
    sums = dot(turned, second[...], NN).astype(BF16)
    for j in range(NX):
        send[j] = sums[j * tile : (j + 1) * tile]


def backward(live, hidden, slope, second, both, keep, send, whole, grads):
    tile, width = both.shape[1] // 2, both.shape[2]
    row = lax.broadcasted_iota(jnp.int32, (tile, width), 0)
    for j in range(NX):
        whole[j * tile : (j + 1) * tile, :] = both[j, :tile]
        given = both[j, tile:].astype(F32)
        alive = jnp.where(row < live[j] * (tile // 4), given, 0.0)
        grads[j * tile : (j + 1) * tile, :] = alive.astype(BF16)
    half = hidden.shape[0] // 2
    step = 320
    for to, base in ((send, half), (keep, 0)):
        for at in range(0, half, step):
            here = slice(base + at, base + at + step)
            to[half + at : half + at + step, :] = dot(hidden[here, :], grads[...], NN).astype(BF16)
            hidden_grad = dot(second[here, :], grads[...], NT)
            pre_grad = (hidden_grad * slope[here, :]).astype(BF16)
            to[at : at + step, :] = dot(pre_grad, whole[...], NN).astype(BF16)


def add_core(keep, got, own, send1, send2, send3):
    half = keep.shape[0] // 2
    part = half // NY
    for m in range(2):
        for j, out in enumerate((own, send1, send2, send3)):
            at = m * half + j * part
            total = keep[at : at + part, :].astype(F32) + got[at : at + part, :].astype(F32)
            out[m * part : (m + 1) * part, :] = total.astype(out.dtype)


def add_y(place, own, got1, got2, got3, out):
    half = own.shape[0] // 2
    part = half // NZ
    small = part // 2
    for m in range(2):
        for jz in range(NZ):
            here = slice(m * half + jz * part, m * half + (jz + 1) * part)
            total = own[here, :] + got1[here, :].astype(F32)
            total = total + (got2[here, :].astype(F32) + got3[here, :].astype(F32))
            to = ((place[0] + jz) % NZ) * NG
            for g in range(NG):
                block = total[g * small : (g + 1) * small].astype(BF16)
                out[to + g, m * small : (m + 1) * small, :] = block


def add_z(got, first, second):
    total = got[0].astype(F32)
    for i in range(1, got.shape[0]):
        total = total + got[i].astype(F32)
    half = total.shape[0] // 2
    first[...] = total[:half]
    second[...] = total[half:]


def project(got, x, shift, wk, wv, out):
    total = (got[0].astype(F32) + got[1].astype(F32)) + (got[2].astype(F32) + got[3].astype(F32))
    states = (x[...].astype(F32) + total + shift[...]).astype(BF16)
    keys = dot(states, wk[...], NN)
    values = dot(states, wv[...], NN).astype(BF16)
    for h in range(KV_HEADS):
        raw = keys[:, h * HD : (h + 1) * HD]
        scale = lax.rsqrt(jnp.mean(raw * raw, axis=-1, keepdims=True) + EPSILON)
        key = (raw * scale).astype(BF16)
        for c in range(NC):
            out[h * NC + c, :, :HD] = key
            out[h * NC + c, :, HD:] = values[:, h * HD : (h + 1) * HD]


def ask(text, weight, out, total):
    k = pl.program_id(0)

    @pl.when(k == 0)
    def _():
        total[...] = jnp.zeros_like(total)

    total[...] += dot(text[...], weight[...], NN)

    @pl.when(k == pl.num_programs(0) - 1)
    def _():
        for h in range(out.shape[1] // HD):
            raw = total[:, h * HD : (h + 1) * HD]
            scale = lax.rsqrt(jnp.mean(raw * raw, axis=-1, keepdims=True) + EPSILON)
            out[:, h * HD : (h + 1) * HD] = (raw * scale).astype(BF16)


def attend(tiles, links, lengths, queries, got, out):
    samples, length, width = out.shape
    heads = width // HD
    images, img_rows = got.shape[:2]
    lane = lax.broadcasted_iota(jnp.int32, (1, 2 * img_rows), 1)
    position = lax.broadcasted_iota(jnp.int32, (length, HD), 0)
    for s in range(samples):
        mine = queries[s * length : (s + 1) * length, :]
        asked = jnp.concatenate([mine[:, h * HD : (h + 1) * HD] for h in range(heads)], axis=0)
        total = jnp.zeros((heads * length, 1), F32)
        mixed = jnp.zeros((heads * length, HD), F32)
        for j in range(0, images, 2):
            keys = jnp.concatenate([got[j, :, :HD], got[j + 1, :, :HD]], axis=0)
            values = jnp.concatenate([got[j, :, HD:], got[j + 1, :, HD:]], axis=0)
            scores = dot(asked, keys, NT) * HD ** (-0.5)
            reach0 = tiles[j] * (img_rows // 4) * links[s, j]
            reach1 = tiles[j + 1] * (img_rows // 4) * links[s, j + 1]
            reach = jnp.where(lane < img_rows, reach0, img_rows + reach1)
            weights = jnp.exp(scores) * jnp.where(lane < reach, 1.0, 0.0)
            total = total + jnp.sum(weights, axis=-1, keepdims=True)
            mixed = mixed + dot(weights.astype(BF16), values, NN)
        mixed = mixed / total
        valid = position < lengths[s]
        for h in range(heads):
            part = jnp.where(valid, mixed[h * length : (h + 1) * length, :], 0.0)
            out[s, :, h * HD : (h + 1) * HD] = part.astype(BF16)


def on_device(
    images,
    ln_gain,
    ln_bias,
    fc1_weight,
    fc1_bias,
    fc2_weight,
    fc2_bias,
    key_weight,
    value_weight,
    text,
    query_weight,
    tiles,
    links,
    lengths,
    state_grads,
):
    zh, x, y, core, grp = (lax.axis_index(a) for a in ("zh", "x", "y", "core", "grp"))
    enc_place = zh * NX + x
    dec_place = y * NC + core
    dec_count = NY * NC
    slots, patch, width = images.shape[1:]
    img_rows = slots * patch
    own_rows = images.reshape(img_rows, width)
    shard = fc1_weight.shape[0]
    share = shard // dec_count
    count = shard * NZ
    wide = width + HD

    spread_rows, piece, terms = local(
        prepare,
        [
            sds((NX, 2 * img_rows, width), BF16),
            sds((2 * share, wide), BF16),
            sds((shard, HD), BF16),
        ],
        (dec_place * share)[None],
        own_rows,
        ln_gain[None],
        ln_bias[None],
        state_grads.reshape(img_rows, width),
        fc1_bias[None],
        fc1_weight,
        fc2_weight,
        scalars=1,
        raw=2,
        scratch=[pltpu.SemaphoreType.DMA((2,))],
    )
    from_zh = [pull(piece, "zh", j) for j in range(1, NZ)]
    rows = lax.all_to_all(spread_rows, "x", split_axis=0, concat_axis=0, tiled=True)
    (joined,) = local(join, [sds((6 * share, wide), BF16)], *from_zh, after=[rows])
    late_weight, *_ = lax.optimization_barrier((query_weight, joined))
    query_full = lax.all_gather(late_weight, ("zh", "x"), axis=0, tiled=True)
    near = [joined] + [pull(joined, "y", j) for j in range(1, NY)]
    pieces = near + [pull(p, "core", 1) for p in near]

    hidden, slope, second, sends = local(
        forward,
        [
            sds((count, NX * img_rows), BF16),
            sds((count, NX * img_rows), F32),
            sds((count, width), BF16),
            sds((NX, img_rows, width), BF16),
        ],
        jnp.stack([y, core]),
        fc1_weight,
        fc2_weight,
        terms,
        *pieces,
        rows,
        scalars=1,
        scratch=[
            pltpu.VMEM((count, width), BF16),
            pltpu.VMEM((count, HD), BF16),
            pltpu.VMEM((NX * img_rows, width), BF16),
        ],
        flops=4 * count * NX * img_rows * width,
        limit=50,
    )
    sums = lax.all_to_all(sends, "x", split_axis=0, concat_axis=0, tiled=True)
    live = lax.dynamic_slice(tiles, (zh * NX, dec_place, grp), (NX, 1, 1)).reshape(NX)

    half = count // 2
    g_keep, g_send = local(
        backward,
        [sds((count, width), BF16), sds((count, width), BF16)],
        live,
        hidden,
        slope,
        second,
        rows,
        scalars=1,
        scratch=[
            pltpu.VMEM((NX * img_rows, width), BF16),
            pltpu.VMEM((NX * img_rows, width), BF16),
        ],
        flops=6 * count * NX * img_rows * width,
        limit=50,
    )
    (send,) = local(
        project,
        [sds((dec_count, img_rows, 2 * HD), BF16)],
        sums,
        own_rows,
        fc2_bias[None],
        key_weight,
        value_weight,
        flops=4 * img_rows * width * KV_HEADS * HD,
    )
    got = lax.all_to_all(send, ("y", "core"), split_axis=0, concat_axis=0, tiled=True)

    g_got = push(g_send, "core", 1)
    part = count // NY
    y_own, *y_sends = local(
        add_core,
        [sds((part, width), F32)] + [sds((part, width), BF16)] * 3,
        g_keep,
        g_got,
        after=[send],
    )
    y_got = [push(y_sends[j - 1], "y", j) for j in range(1, NY)]
    samples, length, deep = text.shape
    mine = query_weight.shape[1]
    grid = 8
    queries = pl.pallas_call(
        ask,
        grid=(grid,),
        in_specs=[
            pl.BlockSpec((samples * length, deep // grid), lambda k: (0, k)),
            pl.BlockSpec((deep // grid, mine), lambda k: (k, 0)),
        ],
        out_specs=pl.BlockSpec((samples * length, mine), lambda k: (0, 0)),
        out_shape=sds((samples * length, mine), BF16),
        scratch_shapes=[pltpu.VMEM((samples * length, mine), F32)],
        compiler_params=pltpu.CompilerParams(vmem_limit_bytes=24 << 20),
        cost_estimate=pl.CostEstimate(
            flops=2 * samples * length * deep * mine,
            transcendentals=0,
            bytes_accessed=2 * deep * (samples * length + mine),
        ),
    )(text.reshape(samples * length, deep), query_full)
    (z_send,) = local(
        add_y,
        [sds((NZ * NG, share, width), BF16)],
        zh[None],
        y_own,
        *y_got,
        scalars=1,
        after=[queries],
    )
    z_got = lax.all_to_all(z_send, ("zh", "grp"), split_axis=0, concat_axis=0, tiled=True)
    (context,) = local(
        attend,
        [sds((samples, length, mine), BF16)],
        tiles[enc_place, :, grp],
        links,
        lengths,
        queries,
        got,
        scalars=3,
        flops=4 * samples * length * mine * dec_count * img_rows,
    )
    fc1_grad, fc2_grad = local(
        add_z, [sds((share // 2, width), F32)] * 2, z_got, after=[context]
    )
    return (context, fc1_grad, fc2_grad)


def solution(mesh):
    fine = Mesh(mesh.devices.reshape(NZ, NX, NY, NC, NG), ("zh", "x", "y", "core", "grp"))
    enc = ("zh", "x")
    dec = ("y", "core")
    in_specs = (
        P(enc + dec + ("grp",), None, None, None),
        P(),
        P(),
        P(enc, None),
        P(enc),
        P(enc, None),
        P(),
        P(),
        P(),
        P(enc + ("grp",), None, None),
        P(enc, dec),
        P(),
        P(enc + ("grp",), None),
        P(enc + ("grp",)),
        P(enc + dec + ("grp",), None, None, None),
    )
    out_specs = (
        P(enc + ("grp",), None, dec),
        P(enc + dec + ("grp",), None),
        P(enc + dec + ("grp",), None),
    )
    return jax.shard_map(
        on_device, mesh=fine, in_specs=in_specs, out_specs=out_specs, check_vma=False
    )
```

profile of v0, /device:TPU:1, one launch (start us, length us, event | category | flops | bytes accessed | tf_op | source)
XLA Modules:
  0.0 239.1 jit_solution(11886754318936486302)
XLA Ops:
  9.3 1.0 copy-done.6
  10.2 1.1 copy-done.10
  11.4 1.1 copy-done.11
  12.5 1.0 copy-done.12
  14.0 1.5 copy-done.5
  16.1 4.8 %all-to-all-start = ((bf16[4,256,1280]{2,1,0:T(8,128)(2,1)}), bf16[4,256,1280]{2,1,0:T(8,128)(2,1)S(1)}, u32[]{:S(2)}, u32[]{:S(2)}) async-start(bf16[4,256,1280]{2,1,0:T(8,128)(2,1)} %copy-done.5), calls=%async_computation | async-start | bytes 5242880 | tf_op jit(solution)/shard_map/all_to_all | solution.py:303
  21.0 3.0 %collective-permute-start.2 = (bf16[80,1408]{1,0:T(8,128)(2,1)S(1)}, bf16[80,1408]{1,0:T(8,128)(2,1)S(1)}, u32[]{:S(2)}, u32[]{:S(2)}) collective-permute-start(bf16[80,1408]{1,0:T(8,128)(2,1)S(1)} %get-tuple-element.19), channel_id=1, source_target_pairs={{192,0},{0,64},{64,128},{128,192},{193,1},{1,65},{65,129},{129,193... | collective-permute-start | bytes 675848 | tf_op jit(solution)/shard_map/ppermute | solution.py:52
  24.0 5.1 %collective-permute-start.1 = (bf16[80,1408]{1,0:T(8,128)(2,1)S(1)}, bf16[80,1408]{1,0:T(8,128)(2,1)S(1)}, u32[]{:S(2)}, u32[]{:S(2)}) collective-permute-start(bf16[80,1408]{1,0:T(8,128)(2,1)S(1)} %get-tuple-element.19), channel_id=1, source_target_pairs={{128,0},{192,64},{0,128},{64,192},{129,1},{193,65},{1,129},{65,193... | collective-permute-start | bytes 675848 | tf_op jit(solution)/shard_map/ppermute | solution.py:52
  29.1 2.4 collective-permute-start
  31.5 2.1 collective-permute-done.2.refs_2_
  33.5 7.9 %collective-permute-done.1.refs_1_ = bf16[80,1408]{1,0:T(8,128)(2,1)S(1)} collective-permute-done((bf16[80,1408]{1,0:T(8,128)(2,1)S(1)}, bf16[80,1408]{1,0:T(8,128)(2,1)S(1)}, u32[]{:S(2)}, u32[]{:S(2)}) %collective-permute-start.1) | collective-permute-done | bytes 225312 | tf_op jit(solution)/shard_map/ppermute | solution.py:52
  42.2 8.0 %collective-permute-done.refs_0_ = bf16[80,1408]{1,0:T(8,128)(2,1)S(1)} collective-permute-done((bf16[80,1408]{1,0:T(8,128)(2,1)S(1)}, bf16[80,1408]{1,0:T(8,128)(2,1)S(1)}, u32[]{:S(2)}, u32[]{:S(2)}) %collective-permute-start) | collective-permute-done | bytes 225312 | tf_op jit(solution)/shard_map/ppermute | solution.py:52
  50.9 0.9 copy-done.15
  51.9 0.9 copy-done.17
  52.9 2.5 %collective-permute-start.5 = (bf16[240,1408]{1,0:T(8,128)(2,1)S(1)}, bf16[240,1408]{1,0:T(8,128)(2,1)}, u32[]{:S(2)}, u32[]{:S(2)}) collective-permute-start(bf16[240,1408]{1,0:T(8,128)(2,1)S(1)} %shard_map.167.refs_4_), channel_id=1, source_target_pairs={{12,0},{0,4},{4,8},{8,12},{13,1},{1,5},{5,9},{9,13},{14,2},{2,6},{... | collective-permute-start | bytes 2027528 | tf_op jit(solution)/shard_map/ppermute | solution.py:52
  55.3 2.6 %collective-permute-start.4 = (bf16[240,1408]{1,0:T(8,128)(2,1)S(1)}, bf16[240,1408]{1,0:T(8,128)(2,1)}, u32[]{:S(2)}, u32[]{:S(2)}) collective-permute-start(bf16[240,1408]{1,0:T(8,128)(2,1)S(1)} %shard_map.167.refs_4_), channel_id=1, source_target_pairs={{8,0},{12,4},{0,8},{4,12},{9,1},{13,5},{1,9},{5,13},{10,2},{14,6},... | collective-permute-start | bytes 2027528 | tf_op jit(solution)/shard_map/ppermute | solution.py:52
  58.0 1.1 collective-permute-start.3
  59.0 2.7 %collective-permute-start.6 = (bf16[240,1408]{1,0:T(8,128)(2,1)S(1)}, bf16[240,1408]{1,0:T(8,128)(2,1)}, u32[]{:S(2)}, u32[]{:S(2)}) collective-permute-start(bf16[240,1408]{1,0:T(8,128)(2,1)S(1)} %shard_map.167.refs_4_), channel_id=1, source_target_pairs={{2,0},{0,2},{3,1},{1,3},{6,4},{4,6},{7,5},{5,7},{10,8},{8,10},{11,... | collective-permute-start | bytes 2027528 | tf_op jit(solution)/shard_map/ppermute | solution.py:52
  61.7 8.6 %collective-permute-done.5.refs_7_ = bf16[240,1408]{1,0:T(8,128)(2,1)} collective-permute-done((bf16[240,1408]{1,0:T(8,128)(2,1)S(1)}, bf16[240,1408]{1,0:T(8,128)(2,1)}, u32[]{:S(2)}, u32[]{:S(2)}) %collective-permute-start.5) | collective-permute-done | bytes 675872 | tf_op jit(solution)/shard_map/ppermute | solution.py:52
  70.3 3.9 %collective-permute-start.9 = (bf16[240,1408]{1,0:T(8,128)(2,1)}, bf16[240,1408]{1,0:T(8,128)(2,1)}, u32[]{:S(2)}, u32[]{:S(2)}) collective-permute-start(bf16[240,1408]{1,0:T(8,128)(2,1)} %collective-permute-done.5.refs_7_), channel_id=1, source_target_pairs={{2,0},{0,2},{3,1},{1,3},{6,4},{4,6},{7,5},{5,7},{10,8},{8,10},{11,... | collective-permute-start | bytes 2027528 | tf_op jit(solution)/shard_map/ppermute | solution.py:52
  74.2 11.7 %collective-permute-done.4.refs_6_ = bf16[240,1408]{1,0:T(8,128)(2,1)} collective-permute-done((bf16[240,1408]{1,0:T(8,128)(2,1)S(1)}, bf16[240,1408]{1,0:T(8,128)(2,1)}, u32[]{:S(2)}, u32[]{:S(2)}) %collective-permute-start.4) | collective-permute-done | bytes 675872 | tf_op jit(solution)/shard_map/ppermute | solution.py:52
  85.9 2.8 %collective-permute-start.8 = (bf16[240,1408]{1,0:T(8,128)(2,1)}, bf16[240,1408]{1,0:T(8,128)(2,1)}, u32[]{:S(2)}, u32[]{:S(2)}) collective-permute-start(bf16[240,1408]{1,0:T(8,128)(2,1)} %collective-permute-done.4.refs_6_), channel_id=1, source_target_pairs={{2,0},{0,2},{3,1},{1,3},{6,4},{4,6},{7,5},{5,7},{10,8},{8,10},{11,... | collective-permute-start | bytes 2027528 | tf_op jit(solution)/shard_map/ppermute | solution.py:52
  88.8 1.9 collective-permute-done.8.refs_10_
  90.8 1.0 collective-permute-done.7.refs_9_
  92.6 10.5 %shard_map.169 = (bf16[1280,512]{1,0:T(8,128)(2,1)}, f32[1280,512]{1,0:T(8,128)}, bf16[1280,1280]{1,0:T(8,128)(2,1)}, bf16[4,128,1280]{2,1,0:T(8,128)(2,1)}) custom-call(s32[2]{0:T(128)S(1)} %pad_add_fusion.refs_0_, bf16[320,1280]{1,0:T(8,128)(2,1)} %refs_1_.2, bf16[320,1280]{1,0:T(8,128)(2,1)} %refs_2_.2, bf16[320,128]{1,0:T(8,128)(2,1)S(1)} %copy-done.19, ...), custom_call_target="tpu_custom_call" | custom-call | flops 3355443200 | bytes 18268168 | tf_op jit(solution)/shard_map/pallas_call | solution.py:35
  103.1 1.7 copy-done.22
  104.9 1.3 copy-done.23
  106.2 10.5 %shard_map.172 = (bf16[1280,1280]{1,0:T(8,128)(2,1)}, bf16[1280,1280]{1,0:T(8,128)(2,1)}) custom-call(s32[4]{0:T(128)S(1)} %dynamic-slice_bitcast_fusion.refs_0_, bf16[1280,512]{1,0:T(8,128)(2,1)S(1)} %copy-done.23, f32[1280,512]{1,0:T(8,128)S(1)} %copy-done.22, bf16[1280,1280]{1,0:T(8,128)(2,1)} %get-tuple-element.26.refs_3_, bf16[4,256,1280]{2,1,0:T(8,128)(2,1)} %copy-done.1), custom_call_target="tpu_custom_call" | custom-call | flops 5033164800 | bytes 16384016 | tf_op jit(solution)/shard_map/pallas_call | solution.py:35
  117.2 3.7 %all-to-all-start.1 = ((bf16[4,128,1280]{2,1,0:T(8,128)(2,1)}), bf16[4,128,1280]{2,1,0:T(8,128)(2,1)S(1)}, u32[]{:S(2)}, u32[]{:S(2)}) async-start(bf16[4,128,1280]{2,1,0:T(8,128)(2,1)} %get-tuple-element.23), calls=%async_computation.1 | async-start | bytes 2621440 | tf_op jit(solution)/shard_map/all_to_all | solution.py:333
  120.9 27.2 %all-to-all-done.1.refs_0_ = bf16[4,128,1280]{2,1,0:T(8,128)(2,1)S(1)} async-done(((bf16[4,128,1280]{2,1,0:T(8,128)(2,1)}), bf16[4,128,1280]{2,1,0:T(8,128)(2,1)S(1)}, u32[]{:S(2)}, u32[]{:S(2)}) %all-to-all-start.1) | async-done | bytes 1310752 | tf_op jit(solution)/shard_map/all_to_all | solution.py:333
  148.2 1.3 copy-done.9
  149.5 1.4 shard_map.170.refs_2_
  151.6 3.8 %shard_map.173 = (f32[320,1280]{1,0:T(8,128)S(1)}, bf16[320,1280]{1,0:T(8,128)(2,1)}, bf16[320,1280]{1,0:T(8,128)(2,1)}, bf16[320,1280]{1,0:T(8,128)(2,1)}) custom-call(bf16[1280,1280]{1,0:T(8,128)(2,1)S(1)} %copy-done.4, bf16[1280,1280]{1,0:T(8,128)(2,1)} %collective-permute-done.10.refs_1_, bf16[8,128,256]{2,1,0:T(8,128)(2,1)} %shard_map.170.refs_2_), custom_call_target="tpu_custom_call" | custom-call | bytes 10649600 | tf_op jit(solution)/shard_map/pallas_call | solution.py:35
  155.4 1.9 collective-permute-start.12
  157.3 1.0 collective-permute-start.13
  158.3 7.0 %all-to-all-start.2 = ((bf16[8,128,256]{2,1,0:T(8,128)(2,1)}), bf16[8,128,256]{2,1,0:T(8,128)(2,1)}, u32[]{:S(2)}, u32[]{:S(2)}) async-start(bf16[8,128,256]{2,1,0:T(8,128)(2,1)} %shard_map.170.refs_2_), calls=%async_computation.2 | async-start | bytes 1048576 | tf_op jit(solution)/shard_map/all_to_all | solution.py:363
  165.3 2.2 all-gather.2.cloned.1.call-done.weight
  167.5 3.4 %copy-done.2 = bf16[8192,512]{1,0:T(8,128)(2,1)S(1)} copy-done((bf16[8192,512]{1,0:T(8,128)(2,1)S(1)}, bf16[8192,512]{1,0:T(8,128)(2,1)}, u32[]{:S(2)}) %copy-start.2) | copy-done | bytes 8388632
  170.9 2.2 copy-done.3
  173.1 4.1 %shard_map.168.refs_3_.refs_5_ = bf16[256,512]{1,0:T(8,128)(2,1)S(1)} custom-call(bf16[256,8192]{1,0:T(8,128)(2,1)S(1)} %bitcast.9, bf16[8192,512]{1,0:T(8,128)(2,1)S(1)} %copy-done.2), custom_call_target="tpu_custom_call" | custom-call | flops 2147483648 | bytes 12582912 | tf_op jit(solution)/shard_map/pallas_call | solution.py:378
  177.2 14.5 %collective-permute-done.12.refs_3_ = bf16[320,1280]{1,0:T(8,128)(2,1)S(1)} collective-permute-done((bf16[320,1280]{1,0:T(8,128)(2,1)}, bf16[320,1280]{1,0:T(8,128)(2,1)S(1)}, u32[]{:S(2)}, u32[]{:S(2)}) %collective-permute-start.12) | collective-permute-done | bytes 819232 | tf_op jit(solution)/shard_map/ppermute | solution.py:57
  191.7 2.9 %collective-permute-done.13.refs_4_ = bf16[320,1280]{1,0:T(8,128)(2,1)} collective-permute-done((bf16[320,1280]{1,0:T(8,128)(2,1)}, bf16[320,1280]{1,0:T(8,128)(2,1)}, u32[]{:S(2)}, u32[]{:S(2)}) %collective-permute-start.13) | collective-permute-done | bytes 819232 | tf_op jit(solution)/shard_map/ppermute | solution.py:57
  194.6 2.5 %shard_map.174 = bf16[8,40,1280]{2,1,0:T(8,128)(2,1)} custom-call(s32[1]{0:T(128)} %bitcast.6.refs_0_, f32[320,1280]{1,0:T(8,128)S(1)} %get-tuple-element.29.refs_1_, bf16[320,1280]{1,0:T(8,128)(2,1)S(1)} %collective-permute-done.11.refs_2_, bf16[320,1280]{1,0:T(8,128)(2,1)S(1)} %collective-permute-done.12.refs_3_, ...), custom_call_target="tpu_custom_call" | custom-call | bytes 4915204 | tf_op jit(solution)/shard_map/pallas_call | solution.py:35
  197.1 2.6 %all-to-all-done.2.refs_4_ = bf16[8,128,256]{2,1,0:T(8,128)(2,1)} async-done(((bf16[8,128,256]{2,1,0:T(8,128)(2,1)}), bf16[8,128,256]{2,1,0:T(8,128)(2,1)}, u32[]{:S(2)}, u32[]{:S(2)}) %all-to-all-start.2) | async-done | bytes 524320 | tf_op jit(solution)/shard_map/all_to_all | solution.py:363
  199.6 9.1 %all-to-all-start.3 = ((bf16[8,40,1280]{2,1,0:T(8,128)(2,1)}), bf16[8,40,1280]{2,1,0:T(8,128)(2,1)S(1)}, u32[]{:S(2)}, u32[]{:S(2)}) async-start(bf16[8,40,1280]{2,1,0:T(8,128)(2,1)} %shard_map.174), calls=%async_computation.3 | async-start | bytes 1638400 | tf_op jit(solution)/shard_map/all_to_all | solution.py:404
  209.1 3.3 %shard_map.171.refs_1_ = bf16[2,128,512]{2,1,0:T(8,128)(2,1)} custom-call(s32[8]{0:T(128)S(1)} %dynamic-slice_reduce_fusion.refs_0_, s32[2,8]{1,0:T(2,128)S(1)} %copy-done.20, s32[2]{0:T(128)S(1)} %copy-done.21, bf16[256,512]{1,0:T(8,128)(2,1)S(1)} %shard_map.168.refs_3_.refs_5_, bf16[8,128,256]{2,1,0:T(8,128)(2,1)} %all-to-all-done.2.refs_4_), custom_call_target="tpu_custom_call" | custom-call | flops 536870912 | bytes 1048680 | tf_op jit(solution)/shard_map/pallas_call | solution.py:35
  212.3 18.2 %all-to-all-done.3.refs_0_ = bf16[8,40,1280]{2,1,0:T(8,128)(2,1)S(1)} async-done(((bf16[8,40,1280]{2,1,0:T(8,128)(2,1)}), bf16[8,40,1280]{2,1,0:T(8,128)(2,1)S(1)}, u32[]{:S(2)}, u32[]{:S(2)}) %all-to-all-start.3) | async-done | bytes 819232 | tf_op jit(solution)/shard_map/all_to_all | solution.py:404
  230.5 0.9 copy-done.13
  (58 shorter events, 8.2 us)
Async XLA Ops:
  7.2 81.6 %copy-start = (s32[16,8,2]{0,2,1:T(2,128)S(1)}, s32[16,8,2]{0,2,1:T(2,128)}, u32[]{:S(2)}) copy-start(s32[16,8,2]{0,2,1:T(2,128)} %param.26) | copy-start | bytes 3076
  9.3 1.0 copy-start.6
  10.2 1.1 copy-start.10
  11.4 1.1 copy-start.11
  12.5 1.0 copy-start.12
  14.0 1.5 copy-start.5
  15.5 0.6 copy-start.18
  16.1 34.8 %all-to-all-start = ((bf16[4,256,1280]{2,1,0:T(8,128)(2,1)}), bf16[4,256,1280]{2,1,0:T(8,128)(2,1)S(1)}, u32[]{:S(2)}, u32[]{:S(2)}) async-start(bf16[4,256,1280]{2,1,0:T(8,128)(2,1)} %copy-done.5), calls=%async_computation | async-start | bytes 5242880 | tf_op jit(solution)/shard_map/all_to_all | solution.py:303
  21.0 146.5 %all-gather.2.cloned.1.call-start = ((), (), s32[]{:S(2)}) async-start(), calls=%async_computation.4 | async-start | bytes 8912896 | tf_op jit(solution)/shard_map/all_gather | solution.py:306
  21.0 12.5 %collective-permute-start.2 = (bf16[80,1408]{1,0:T(8,128)(2,1)S(1)}, bf16[80,1408]{1,0:T(8,128)(2,1)S(1)}, u32[]{:S(2)}, u32[]{:S(2)}) collective-permute-start(bf16[80,1408]{1,0:T(8,128)(2,1)S(1)} %get-tuple-element.19), channel_id=1, source_target_pairs={{192,0},{0,64},{64,128},{128,192},{193,1},{1,65},{65,129},{129,193... | collective-permute-start | bytes 675848 | tf_op jit(solution)/shard_map/ppermute | solution.py:52
  24.0 17.5 %collective-permute-start.1 = (bf16[80,1408]{1,0:T(8,128)(2,1)S(1)}, bf16[80,1408]{1,0:T(8,128)(2,1)S(1)}, u32[]{:S(2)}, u32[]{:S(2)}) collective-permute-start(bf16[80,1408]{1,0:T(8,128)(2,1)S(1)} %get-tuple-element.19), channel_id=1, source_target_pairs={{128,0},{192,64},{0,128},{64,192},{129,1},{193,65},{1,129},{65,193... | collective-permute-start | bytes 675848 | tf_op jit(solution)/shard_map/ppermute | solution.py:52
  29.1 21.0 %collective-permute-start = (bf16[80,1408]{1,0:T(8,128)(2,1)S(1)}, bf16[80,1408]{1,0:T(8,128)(2,1)S(1)}, u32[]{:S(2)}, u32[]{:S(2)}) collective-permute-start(bf16[80,1408]{1,0:T(8,128)(2,1)S(1)} %get-tuple-element.19), channel_id=1, source_target_pairs={{64,0},{128,64},{192,128},{0,192},{65,1},{129,65},{193,129},{1,193... | collective-permute-start | bytes 675848 | tf_op jit(solution)/shard_map/ppermute | solution.py:52
  41.5 0.7 copy-start.14
  50.1 0.7 copy-start.16
  50.9 0.9 copy-start.15
  51.9 0.9 copy-start.17
  52.8 38.9 %copy-start.1 = (bf16[4,256,1280]{2,1,0:T(8,128)(2,1)}, bf16[4,256,1280]{2,1,0:T(8,128)(2,1)S(1)}, u32[]{:S(2)}) copy-start(bf16[4,256,1280]{2,1,0:T(8,128)(2,1)S(1)} %all-to-all-done.refs_3_.refs_12_.refs_4_) | copy-start | bytes 7864324
  52.9 17.4 %collective-permute-start.5 = (bf16[240,1408]{1,0:T(8,128)(2,1)S(1)}, bf16[240,1408]{1,0:T(8,128)(2,1)}, u32[]{:S(2)}, u32[]{:S(2)}) collective-permute-start(bf16[240,1408]{1,0:T(8,128)(2,1)S(1)} %shard_map.167.refs_4_), channel_id=1, source_target_pairs={{12,0},{0,4},{4,8},{8,12},{13,1},{1,5},{5,9},{9,13},{14,2},{2,6},{... | collective-permute-start | bytes 2027528 | tf_op jit(solution)/shard_map/ppermute | solution.py:52
  55.3 30.5 %collective-permute-start.4 = (bf16[240,1408]{1,0:T(8,128)(2,1)S(1)}, bf16[240,1408]{1,0:T(8,128)(2,1)}, u32[]{:S(2)}, u32[]{:S(2)}) collective-permute-start(bf16[240,1408]{1,0:T(8,128)(2,1)S(1)} %shard_map.167.refs_4_), channel_id=1, source_target_pairs={{8,0},{12,4},{0,8},{4,12},{9,1},{13,5},{1,9},{5,13},{10,2},{14,6},... | collective-permute-start | bytes 2027528 | tf_op jit(solution)/shard_map/ppermute | solution.py:52
  58.0 30.7 %collective-permute-start.3 = (bf16[240,1408]{1,0:T(8,128)(2,1)S(1)}, bf16[240,1408]{1,0:T(8,128)(2,1)}, u32[]{:S(2)}, u32[]{:S(2)}) collective-permute-start(bf16[240,1408]{1,0:T(8,128)(2,1)S(1)} %shard_map.167.refs_4_), channel_id=1, source_target_pairs={{4,0},{8,4},{12,8},{0,12},{5,1},{9,5},{13,9},{1,13},{6,2},{10,6},{... | collective-permute-start | bytes 2027528 | tf_op jit(solution)/shard_map/ppermute | solution.py:52
  59.0 29.8 %collective-permute-start.6 = (bf16[240,1408]{1,0:T(8,128)(2,1)S(1)}, bf16[240,1408]{1,0:T(8,128)(2,1)}, u32[]{:S(2)}, u32[]{:S(2)}) collective-permute-start(bf16[240,1408]{1,0:T(8,128)(2,1)S(1)} %shard_map.167.refs_4_), channel_id=1, source_target_pairs={{2,0},{0,2},{3,1},{1,3},{6,4},{4,6},{7,5},{5,7},{10,8},{8,10},{11,... | collective-permute-start | bytes 2027528 | tf_op jit(solution)/shard_map/ppermute | solution.py:52
  70.3 18.5 %collective-permute-start.9 = (bf16[240,1408]{1,0:T(8,128)(2,1)}, bf16[240,1408]{1,0:T(8,128)(2,1)}, u32[]{:S(2)}, u32[]{:S(2)}) collective-permute-start(bf16[240,1408]{1,0:T(8,128)(2,1)} %collective-permute-done.5.refs_7_), channel_id=1, source_target_pairs={{2,0},{0,2},{3,1},{1,3},{6,4},{4,6},{7,5},{5,7},{10,8},{8,10},{11,... | collective-permute-start | bytes 2027528 | tf_op jit(solution)/shard_map/ppermute | solution.py:52
  85.9 4.9 %collective-permute-start.8 = (bf16[240,1408]{1,0:T(8,128)(2,1)}, bf16[240,1408]{1,0:T(8,128)(2,1)}, u32[]{:S(2)}, u32[]{:S(2)}) collective-permute-start(bf16[240,1408]{1,0:T(8,128)(2,1)} %collective-permute-done.4.refs_6_), channel_id=1, source_target_pairs={{2,0},{0,2},{3,1},{1,3},{6,4},{4,6},{7,5},{5,7},{10,8},{8,10},{11,... | collective-permute-start | bytes 2027528 | tf_op jit(solution)/shard_map/ppermute | solution.py:52
  88.7 3.1 %collective-permute-start.7 = (bf16[240,1408]{1,0:T(8,128)(2,1)}, bf16[240,1408]{1,0:T(8,128)(2,1)}, u32[]{:S(2)}, u32[]{:S(2)}) collective-permute-start(bf16[240,1408]{1,0:T(8,128)(2,1)} %collective-permute-done.3.refs_5_), channel_id=1, source_target_pairs={{2,0},{0,2},{3,1},{1,3},{6,4},{4,6},{7,5},{5,7},{10,8},{8,10},{11,... | collective-permute-start | bytes 2027528 | tf_op jit(solution)/shard_map/ppermute | solution.py:52
  91.7 0.9 copy-start.19
  103.1 1.7 copy-start.22
  104.9 1.3 copy-start.23
  116.7 4.2 %copy-start.24 = (f32[1280]{0:T(1024)S(1)}, f32[1280]{0:T(1024)}, u32[]{:S(2)}) copy-start(f32[1280]{0:T(1024)} %param.21) | copy-start | bytes 15364
  116.7 31.5 %copy-start.7 = (bf16[1,4,32,1280]{3,2,1,0:T(8,128)(2,1)S(1)}, bf16[1,4,32,1280]{3,2,1,0:T(8,128)(2,1)}, u32[]{:S(2)}) copy-start(bf16[1,4,32,1280]{3,2,1,0:T(8,128)(2,1)} %param.15) | copy-start | bytes 983044
  116.7 31.5 %copy-start.8 = (bf16[1280,512]{1,0:T(8,128)(2,1)S(1)}, bf16[1280,512]{1,0:T(8,128)(2,1)}, u32[]{:S(2)}) copy-start(bf16[1280,512]{1,0:T(8,128)(2,1)} %refs_3_.1) | copy-start | bytes 3932164
  116.7 34.2 %collective-permute-start.10 = (bf16[1280,1280]{1,0:T(8,128)(2,1)}, bf16[1280,1280]{1,0:T(8,128)(2,1)}, u32[]{:S(2)}, u32[]{:S(2)}) collective-permute-start(bf16[1280,1280]{1,0:T(8,128)(2,1)} %get-tuple-element.28), channel_id=1, source_target_pairs={{0,2},{2,0},{1,3},{3,1},{4,6},{6,4},{5,7},{7,5},{8,10},{10,8},{9,1... | collective-permute-start | bytes 9830408 | tf_op jit(solution)/shard_map/ppermute | solution.py:57
  117.2 31.0 %all-to-all-start.1 = ((bf16[4,128,1280]{2,1,0:T(8,128)(2,1)}), bf16[4,128,1280]{2,1,0:T(8,128)(2,1)S(1)}, u32[]{:S(2)}, u32[]{:S(2)}) async-start(bf16[4,128,1280]{2,1,0:T(8,128)(2,1)} %get-tuple-element.23), calls=%async_computation.1 | async-start | bytes 2621440 | tf_op jit(solution)/shard_map/all_to_all | solution.py:333
  148.2 1.3 copy-start.9
  149.5 2.1 copy-start.4
  155.4 21.8 %collective-permute-start.11 = (bf16[320,1280]{1,0:T(8,128)(2,1)}, bf16[320,1280]{1,0:T(8,128)(2,1)S(1)}, u32[]{:S(2)}, u32[]{:S(2)}) collective-permute-start(bf16[320,1280]{1,0:T(8,128)(2,1)} %get-tuple-element.30), channel_id=1, source_target_pairs={{0,4},{4,8},{8,12},{12,0},{1,5},{5,9},{9,13},{13,1},{2,6},{6,10},{... | collective-permute-start | bytes 2457608 | tf_op jit(solution)/shard_map/ppermute | solution.py:57
  155.4 36.2 %collective-permute-start.12 = (bf16[320,1280]{1,0:T(8,128)(2,1)}, bf16[320,1280]{1,0:T(8,128)(2,1)S(1)}, u32[]{:S(2)}, u32[]{:S(2)}) collective-permute-start(bf16[320,1280]{1,0:T(8,128)(2,1)} %get-tuple-element.31), channel_id=1, source_target_pairs={{0,8},{4,12},{8,0},{12,4},{1,9},{5,13},{9,1},{13,5},{2,10},{6,14},... | collective-permute-start | bytes 2457608 | tf_op jit(solution)/shard_map/ppermute | solution.py:57
  157.3 37.2 %collective-permute-start.13 = (bf16[320,1280]{1,0:T(8,128)(2,1)}, bf16[320,1280]{1,0:T(8,128)(2,1)}, u32[]{:S(2)}, u32[]{:S(2)}) collective-permute-start(bf16[320,1280]{1,0:T(8,128)(2,1)} %get-tuple-element.32), channel_id=1, source_target_pairs={{0,12},{4,0},{8,4},{12,8},{1,13},{5,1},{9,5},{13,9},{2,14},{6,2},{... | collective-permute-start | bytes 2457608 | tf_op jit(solution)/shard_map/ppermute | solution.py:57
  158.3 41.4 %all-to-all-start.2 = ((bf16[8,128,256]{2,1,0:T(8,128)(2,1)}), bf16[8,128,256]{2,1,0:T(8,128)(2,1)}, u32[]{:S(2)}, u32[]{:S(2)}) async-start(bf16[8,128,256]{2,1,0:T(8,128)(2,1)} %shard_map.170.refs_2_), calls=%async_computation.2 | async-start | bytes 1048576 | tf_op jit(solution)/shard_map/all_to_all | solution.py:363
  167.5 3.4 %copy-start.2 = (bf16[8192,512]{1,0:T(8,128)(2,1)S(1)}, bf16[8192,512]{1,0:T(8,128)(2,1)}, u32[]{:S(2)}) copy-start(bf16[8192,512]{1,0:T(8,128)(2,1)} %all-gather.2.cloned.1.call-done.weight) | copy-start | bytes 25165828
  170.9 2.2 copy-start.3
  194.6 14.5 %copy-start.20 = (s32[2,8]{1,0:T(2,128)S(1)}, s32[2,8]{1,0:T(2,128)}, u32[]{:S(2)}) copy-start(s32[2,8]{1,0:T(2,128)} %refs_1_.3) | copy-start | bytes 196
  194.6 14.5 %copy-start.21 = (s32[2]{0:T(128)S(1)}, s32[2]{0:T(128)}, u32[]{:S(2)}) copy-start(s32[2]{0:T(128)} %refs_2_.3) | copy-start | bytes 28
  199.6 30.9 %all-to-all-start.3 = ((bf16[8,40,1280]{2,1,0:T(8,128)(2,1)}), bf16[8,40,1280]{2,1,0:T(8,128)(2,1)S(1)}, u32[]{:S(2)}, u32[]{:S(2)}) async-start(bf16[8,40,1280]{2,1,0:T(8,128)(2,1)} %shard_map.174), calls=%async_computation.3 | async-start | bytes 1638400 | tf_op jit(solution)/shard_map/all_to_all | solution.py:404
  230.5 1.0 copy-start.13
Sparse Core Ops, SparseCore 0:
  53.0 114.4 all-gather.1
where the time goes:
time: 242 us; the launch traced here: 239 us
  waiting for transfers between devices  109 us (45%)
  starting transfers between devices  54 us (22%)
  Pallas kernels  37.4 us (15%)
  local copies, waits for them, and re-layouts  24.6 us (10%)
  between operations  14.2 us (6%)
    ppermute x10, waiting for transfers between devices, pull(): return lax.ppermute(array, axis, [((i + step) % n, i) for i in range(n)])  41.1 us
    pallas_call x9, Pallas kernels, local(): pl.pallas_call(ordered, out_shape=tuple(outs), in_specs=in_specs, out_spe...  33.3 us
    all_to_all x1, waiting for transfers between devices, on_device(): sums = lax.all_to_all(sends, 'x', split_axis=0, concat_axis=0, tiled=True)  27.2 us
    ppermute x10, starting transfers between devices, pull(): return lax.ppermute(array, axis, [((i + step) % n, i) for i in range(n)])  26.1 us
    unnamed x50, local copies, waits for them, and re-layouts  22.2 us
    all_to_all x1, waiting for transfers between devices, on_device(): lax.all_to_all(z_send, ('zh', 'grp'), split_axis=0, concat_axis=0, tiled=...  18.2 us
    ppermute x4, waiting for transfers between devices, push(): return lax.ppermute(array, axis, [(i, (i + step) % n) for i in range(n)])  17.4 us
    all_to_all x1, starting transfers between devices, on_device(): lax.all_to_all(z_send, ('zh', 'grp'), split_axis=0, concat_axis=0, tiled=...  9.11 us
  transfers between devices with their start and end apart: 19, of which 14 were waited for; matrix products, arithmetic and copies ran while one was open for 0% of the time, Pallas kernels for 15%

commit v1 on v0

--- a/solution.py
+++ b/solution.py
@@ -31,7 +31,8 @@
     moved += sum(o.size * o.dtype.itemsize for o in outs)
     in_specs = [pl.BlockSpec(memory_space=pltpu.SMEM)] * scalars
     in_specs += [pl.BlockSpec(memory_space=pltpu.VMEM)] * (len(args) - scalars - raw)
-    in_specs += [pl.BlockSpec(memory_space=pl.ANY)] * (raw + len(after))
+    in_specs += [pl.BlockSpec(memory_space=pltpu.MemorySpace.HBM)] * raw
+    in_specs += [pl.BlockSpec(memory_space=pl.ANY)] * len(after)
     return pl.pallas_call(
         ordered,
         out_shape=tuple(outs),
@@ -57,28 +58,26 @@
     return lax.ppermute(array, axis, [(i, (i + step) % n) for i in range(n)])
 
 
-def prepare(place, x, gain, shift, grads, b1, w1, w2, both, piece, terms, sem):
-    width = x.shape[1]
+def prepare(place, gain, shift, b1, images, grads, w1, w2, both, piece, terms, x, sem):
+    tile, width = x.shape
     share = piece.shape[0] // 2
     start = pl.multiple_of(place[0], 8)
+    first_in = pltpu.make_async_copy(images, x, sem.at[0])
+    first_in.start()
     copies = [
         pltpu.make_async_copy(
-            w.at[pl.ds(start, share), :], piece.at[pl.ds(m * share, share), pl.ds(0, width)], sem.at[m]
+            w.at[pl.ds(start, share), :],
+            piece.at[pl.ds(m * share, share), pl.ds(0, width)],
+            sem.at[1 + m],
         )
         for m, w in enumerate((w1, w2))
     ]
+    copies += [
+        pltpu.make_async_copy(grads, both.at[j, pl.ds(tile, tile), :], sem.at[3 + j])
+        for j in range(NX)
+    ]
     for copy in copies:
         copy.start()
-    tile = x.shape[0]
-    values = x[...].astype(F32)
-    middle = jnp.mean(values, axis=-1, keepdims=True)
-    centered = values - middle
-    spread = jnp.mean(centered * centered, axis=-1, keepdims=True)
-    normed = (centered * lax.rsqrt(spread + EPSILON) * gain[...] + shift[...]).astype(BF16)
-    given = grads[...]
-    for j in range(NX):
-        both[j, :tile] = normed
-        both[j, tile:] = given
     count = b1.shape[1]
     row = lax.broadcasted_iota(jnp.int32, (count, count), 0)
     lane = lax.broadcasted_iota(jnp.int32, (count, count), 1)
@@ -92,6 +91,14 @@
     ).astype(BF16)
     piece[:share, width:] = terms[pl.ds(start, share), :]
     piece[share:, width:] = jnp.zeros((share, piece.shape[1] - width), BF16)
+    first_in.wait()
+    values = x[...].astype(F32)
+    middle = jnp.mean(values, axis=-1, keepdims=True)
+    centered = values - middle
+    spread = jnp.mean(centered * centered, axis=-1, keepdims=True)
+    normed = (centered * lax.rsqrt(spread + EPSILON) * gain[...] + shift[...]).astype(BF16)
+    for j in range(NX):
+        both[j, :tile] = normed
     for copy in copies:
         copy.wait()
 
@@ -103,30 +110,36 @@
     out[2 * n :, :] = c[...]
 
 
-def forward(place, w1, w2, terms, *refs):
-    pieces, both = refs[:8], refs[8]
-    hidden, slope, second, send, first, bias, whole = refs[9:]
+def mlp(place, live, w1, w2, terms, *refs):
+    pieces, mine, other = refs[:4], refs[4], refs[5]
+    send, own, out1, out2, out3 = refs[6:11]
+    first, second, bias, whole, grads, hidden, slope = refs[11:]
     share = pieces[0].shape[0] // 6
     width = w1.shape[1]
-    tile = both.shape[1] // 2
-    for j in range(NX):
-        whole[j * tile : (j + 1) * tile, :] = both[j, :tile]
-    for jc in range(NC):
-        for jy in range(NY):
-            at = (jc * NY + jy) * NZ * share
-            peer = ((place[0] + jy) % NY) * NC + (place[1] + jc) % NC
-            start = pl.multiple_of(peer * share, 8)
-            first[at : at + share, :] = w1[pl.ds(start, share), :]
-            second[at : at + share, :] = w2[pl.ds(start, share), :]
-            bias[at : at + share, :] = terms[pl.ds(start, share), :]
-            piece = pieces[jc * NY + jy]
-            for jz in range(1, NZ):
-                to, own = at + jz * share, (jz - 1) * 2 * share
-                first[to : to + share, :] = piece[own : own + share, :width]
-                second[to : to + share, :] = piece[own + share : own + 2 * share, :width]
-                bias[to : to + share, :] = piece[own : own + share, width:]
+    tile = mine.shape[1] // 2
+    row = lax.broadcasted_iota(jnp.int32, (tile, width), 0)
+    for c, both in enumerate((mine, other)):
+        for j in range(NX):
+            here = slice((c * NX + j) * tile, (c * NX + j + 1) * tile)
+            whole[here, :] = both[j, :tile]
+            given = both[j, tile:].astype(F32)
+            alive = jnp.where(row < live[c * NX + j] * (tile // 4), given, 0.0)
+            grads[here, :] = alive.astype(BF16)
+    for jy in range(NY):
+        at = jy * NZ * share
+        peer = ((place[0] + jy) % NY) * NC + place[1]
+        start = pl.multiple_of(peer * share, 8)
+        first[at : at + share, :] = w1[pl.ds(start, share), :]
+        second[at : at + share, :] = w2[pl.ds(start, share), :]
+        bias[at : at + share, :] = terms[pl.ds(start, share), :]
+        piece = pieces[jy]
+        for jz in range(1, NZ):
+            to, from_ = at + jz * share, (jz - 1) * 2 * share
+            first[to : to + share, :] = piece[from_ : from_ + share, :width]
+            second[to : to + share, :] = piece[from_ + share : from_ + 2 * share, :width]
+            bias[to : to + share, :] = piece[from_ : from_ + share, width:]
     count = first.shape[0]
-    step = 256
+    step = count // NY
     for at in range(0, count, step):
         pre = dot(first[at : at + step, :], whole[...], NT)
         pre = pre + jnp.sum(bias[at : at + step, :].astype(F32), axis=1, keepdims=True)
@@ -134,38 +147,16 @@
         hidden[at : at + step, :] = (pre * phi).astype(BF16)
         slope[at : at + step, :] = phi + pre * jnp.exp(-0.5 * pre * pre) * 0.3989422804014327
     turned = jnp.swapaxes(hidden[...], 0, 1)
-    sums = dot(turned, second[...], NN).astype(BF16)
-    for j in range(NX):
-        send[j] = sums[j * tile : (j + 1) * tile]
-
-
-def backward(live, hidden, slope, second, both, keep, send, whole, grads):
-    tile, width = both.shape[1] // 2, both.shape[2]
-    row = lax.broadcasted_iota(jnp.int32, (tile, width), 0)
-    for j in range(NX):
-        whole[j * tile : (j + 1) * tile, :] = both[j, :tile]
-        given = both[j, tile:].astype(F32)
-        alive = jnp.where(row < live[j] * (tile // 4), given, 0.0)
-        grads[j * tile : (j + 1) * tile, :] = alive.astype(BF16)
-    half = hidden.shape[0] // 2
-    step = 320
-    for to, base in ((send, half), (keep, 0)):
-        for at in range(0, half, step):
-            here = slice(base + at, base + at + step)
-            to[half + at : half + at + step, :] = dot(hidden[here, :], grads[...], NN).astype(BF16)
-            hidden_grad = dot(second[here, :], grads[...], NT)
-            pre_grad = (hidden_grad * slope[here, :]).astype(BF16)
-            to[at : at + step, :] = dot(pre_grad, whole[...], NN).astype(BF16)
-
-
-def add_core(keep, got, own, send1, send2, send3):
-    half = keep.shape[0] // 2
-    part = half // NY
-    for m in range(2):
-        for j, out in enumerate((own, send1, send2, send3)):
-            at = m * half + j * part
-            total = keep[at : at + part, :].astype(F32) + got[at : at + part, :].astype(F32)
-            out[m * part : (m + 1) * part, :] = total.astype(out.dtype)
+    for c in range(NC):
+        for j in range(NX):
+            here = slice((c * NX + j) * tile, (c * NX + j + 1) * tile)
+            part = dot(turned[here], second[...], NN).astype(BF16)
+            send[j * NC + (place[1] + c) % NC] = part
+    for jy, out in enumerate((own, out1, out2, out3)):
+        here = slice(jy * step, (jy + 1) * step)
+        out[step:, :] = dot(hidden[here, :], grads[...], NN).astype(out.dtype)
+        pre_grad = (dot(second[here, :], grads[...], NT) * slope[here, :]).astype(BF16)
+        out[:step, :] = dot(pre_grad, whole[...], NN).astype(out.dtype)
 
 
 def add_y(place, own, got1, got2, got3, out):
@@ -193,7 +184,9 @@
 
 
 def project(got, x, shift, wk, wv, out):
-    total = (got[0].astype(F32) + got[1].astype(F32)) + (got[2].astype(F32) + got[3].astype(F32))
+    total = got[0].astype(F32)
+    for i in range(1, got.shape[0]):
+        total = total + got[i].astype(F32)
     states = (x[...].astype(F32) + total + shift[...]).astype(BF16)
     keys = dot(states, wk[...], NN)
     values = dot(states, wv[...], NN).astype(BF16)
@@ -277,7 +270,6 @@
     own_rows = images.reshape(img_rows, width)
     shard = fc1_weight.shape[0]
     share = shard // dec_count
-    count = shard * NZ
     wide = width + HD
 
     spread_rows, piece, terms = local(
@@ -288,68 +280,67 @@
             sds((shard, HD), BF16),
         ],
         (dec_place * share)[None],
-        own_rows,
         ln_gain[None],
         ln_bias[None],
+        fc1_bias[None],
+        own_rows,
         state_grads.reshape(img_rows, width),
-        fc1_bias[None],
         fc1_weight,
         fc2_weight,
         scalars=1,
-        raw=2,
-        scratch=[pltpu.SemaphoreType.DMA((2,))],
+        raw=4,
+        scratch=[pltpu.VMEM((img_rows, width), BF16), pltpu.SemaphoreType.DMA((3 + NX,))],
     )
     from_zh = [pull(piece, "zh", j) for j in range(1, NZ)]
     rows = lax.all_to_all(spread_rows, "x", split_axis=0, concat_axis=0, tiled=True)
     (joined,) = local(join, [sds((6 * share, wide), BF16)], *from_zh, after=[rows])
     late_weight, *_ = lax.optimization_barrier((query_weight, joined))
     query_full = lax.all_gather(late_weight, ("zh", "x"), axis=0, tiled=True)
-    near = [joined] + [pull(joined, "y", j) for j in range(1, NY)]
-    pieces = near + [pull(p, "core", 1) for p in near]
-
-    hidden, slope, second, sends = local(
-        forward,
+    pieces = [joined] + [pull(joined, "y", j) for j in range(1, NY)]
+    other_rows = pull(rows, "core", 1)
+
+    column = lax.dynamic_slice(tiles, (zh * NX, 0, grp), (NX, dec_count, 1))
+    column = column.reshape(NX, NY, NC)
+    near = lax.dynamic_slice_in_dim(column, y, 1, 1)[:, 0]
+    live = jnp.concatenate(
         [
-            sds((count, NX * img_rows), BF16),
-            sds((count, NX * img_rows), F32),
-            sds((count, width), BF16),
-            sds((NX, img_rows, width), BF16),
-        ],
+            lax.dynamic_slice_in_dim(near, core, 1, 1)[:, 0],
+            lax.dynamic_slice_in_dim(near, 1 - core, 1, 1)[:, 0],
+        ]
+    )
+    count = shard * NZ // NC
+    total_rows = NX * NC * img_rows
+    part = 2 * count // NY
+    sends, y_own, *y_sends = local(
+        mlp,
+        [
+            sds((NX * NC, img_rows, width), BF16),
+            sds((part, width), F32),
+        ]
+        + [sds((part, width), BF16)] * 3,
         jnp.stack([y, core]),
+        live,
         fc1_weight,
         fc2_weight,
         terms,
         *pieces,
         rows,
-        scalars=1,
+        other_rows,
+        scalars=2,
         scratch=[
             pltpu.VMEM((count, width), BF16),
+            pltpu.VMEM((count, width), BF16),
             pltpu.VMEM((count, HD), BF16),
-            pltpu.VMEM((NX * img_rows, width), BF16),
+            pltpu.VMEM((total_rows, width), BF16),
+            pltpu.VMEM((total_rows, width), BF16),
+            pltpu.VMEM((count, total_rows), BF16),
+            pltpu.VMEM((count, total_rows), F32),
         ],
-        flops=4 * count * NX * img_rows * width,
+        flops=10 * count * total_rows * width,
         limit=50,
     )
-    sums = lax.all_to_all(sends, "x", split_axis=0, concat_axis=0, tiled=True)
-    live = lax.dynamic_slice(tiles, (zh * NX, dec_place, grp), (NX, 1, 1)).reshape(NX)
-
-    half = count // 2
-    g_keep, g_send = local(
-        backward,
-        [sds((count, width), BF16), sds((count, width), BF16)],
-        live,
-        hidden,
-        slope,
-        second,
-        rows,
-        scalars=1,
-        scratch=[
-            pltpu.VMEM((NX * img_rows, width), BF16),
-            pltpu.VMEM((NX * img_rows, width), BF16),
-        ],
-        flops=6 * count * NX * img_rows * width,
-        limit=50,
-    )
+    y_got = [push(y_sends[j - 1], "y", j) for j in range(1, NY)]
+    sums = lax.all_to_all(sends, ("x", "core"), split_axis=0, concat_axis=0, tiled=True)
     (send,) = local(
         project,
         [sds((dec_count, img_rows, 2 * HD), BF16)],
@@ -362,16 +353,6 @@
     )
     got = lax.all_to_all(send, ("y", "core"), split_axis=0, concat_axis=0, tiled=True)
 
-    g_got = push(g_send, "core", 1)
-    part = count // NY
-    y_own, *y_sends = local(
-        add_core,
-        [sds((part, width), F32)] + [sds((part, width), BF16)] * 3,
-        g_keep,
-        g_got,
-        after=[send],
-    )
-    y_got = [push(y_sends[j - 1], "y", j) for j in range(1, NY)]
     samples, length, deep = text.shape
     mine = query_weight.shape[1]
     grid = 8
@@ -399,7 +380,6 @@
         y_own,
         *y_got,
         scalars=1,
-        after=[queries],
     )
     z_got = lax.all_to_all(z_send, ("zh", "grp"), split_axis=0, concat_axis=0, tiled=True)
     (context,) = local(

time: 242 us -> 226 us (0.934)
  starting transfers between devices: 54 us -> 39.1 us
  waiting for transfers between devices: 109 us -> 117 us
  Pallas kernels: 37.4 us -> 30.2 us
    all_to_all x1, waiting for transfers between devices: 27.2 us -> 48.9 us  [on_device(): lax.all_to_all(sends, ('x', 'core'), split_axis=0, concat_axis=0, tiled=T...]
    ppermute x4 -> x3, waiting for transfers between devices: 17.4 us -> 0.01 us  [push(): return lax.ppermute(array, axis, [(i, (i + step) % n) for i in range(n)])]
    ppermute x10 -> x7, starting transfers between devices: 26.1 us -> 16.1 us  [pull(): return lax.ppermute(array, axis, [((i + step) % n, i) for i in range(n)])]
    pallas_call x9 -> x7, Pallas kernels: 33.3 us -> 26.1 us  [local(): pl.pallas_call(ordered, out_shape=tuple(outs), in_specs=in_specs, out_spe...]
    all_to_all x1, waiting for transfers between devices: 18.2 us -> 11.4 us  [on_device(): lax.all_to_all(z_send, ('zh', 'grp'), split_axis=0, concat_axis=0, tiled=...]
    all_to_all x1, waiting for transfers between devices: 0.12 us -> 6.32 us  [on_device(): lax.all_to_all(spread_rows, 'x', split_axis=0, concat_axis=0, tiled=True)]
    ppermute x10 -> x7, waiting for transfers between devices: 41.1 us -> 44.9 us  [pull(): return lax.ppermute(array, axis, [((i + step) % n, i) for i in range(n)])]
    all_to_all x1, starting transfers between devices: 6.98 us -> 4.43 us  [on_device(): lax.all_to_all(send, ('y', 'core'), split_axis=0, concat_axis=0, tiled=True)]
  transfers between devices with their start and end apart: 19 -> 15, of which waited for: 14 -> 9; matrix products, arithmetic and copies ran while one was open for 0% -> 0% of each run, Pallas kernels for 15% -> 13%
where the time goes in v1:
time: 226 us; the launch traced here: 225 us
  waiting for transfers between devices  117 us (52%)
  starting transfers between devices  39.1 us (17%)
  Pallas kernels  30.2 us (13%)
  local copies, waits for them, and re-layouts  24.5 us (11%)
  between operations  14.2 us (6%)
    all_to_all x1, waiting for transfers between devices, on_device(): lax.all_to_all(sends, ('x', 'core'), split_axis=0, concat_axis=0, tiled=T...  48.9 us
    ppermute x7, waiting for transfers between devices, pull(): return lax.ppermute(array, axis, [((i + step) % n, i) for i in range(n)])  44.9 us
    pallas_call x7, Pallas kernels, local(): pl.pallas_call(ordered, out_shape=tuple(outs), in_specs=in_specs, out_spe...  26.1 us
    unnamed x48, local copies, waits for them, and re-layouts  22 us
    ppermute x7, starting transfers between devices, pull(): return lax.ppermute(array, axis, [((i + step) % n, i) for i in range(n)])  16.1 us
    all_to_all x1, waiting for transfers between devices, on_device(): lax.all_to_all(z_send, ('zh', 'grp'), split_axis=0, concat_axis=0, tiled=...  11.4 us
    all_to_all x1, starting transfers between devices, on_device(): lax.all_to_all(z_send, ('zh', 'grp'), split_axis=0, concat_axis=0, tiled=...  6.88 us
    all_to_all x1, waiting for transfers between devices, on_device(): lax.all_to_all(spread_rows, 'x', split_axis=0, concat_axis=0, tiled=True)  6.32 us
  transfers between devices with their start and end apart: 15, of which 9 were waited for; matrix products, arithmetic and copies ran while one was open for 0% of the time, Pallas kernels for 13%

profile of v1, /device:TPU:1, one launch (start us, length us, event | category | flops | bytes accessed | tf_op | source)
XLA Modules:
  0.0 224.7 jit_solution(10020392744040383786)
XLA Ops:
  7.2 0.7 broadcast_in_dim.19.refs_1_
  7.9 0.7 broadcast_in_dim.20.refs_2_
  8.6 0.7 broadcast_in_dim.21.refs_3_
  9.3 1.0 copy-done.6
  10.2 1.1 copy-done.10
  11.4 1.1 copy-done.11
  12.5 1.0 copy-done.12
  13.5 1.1 shard_map.166
  14.6 1.5 copy-done.4
  16.7 4.8 %all-to-all-start = ((bf16[4,256,1280]{2,1,0:T(8,128)(2,1)}), bf16[4,256,1280]{2,1,0:T(8,128)(2,1)S(1)}, u32[]{:S(2)}, u32[]{:S(2)}) async-start(bf16[4,256,1280]{2,1,0:T(8,128)(2,1)} %copy-done.4), calls=%async_computation | async-start | bytes 5242880 | tf_op jit(solution)/shard_map/all_to_all | solution.py:295
  21.5 6.0 %collective-permute-start = (bf16[80,1408]{1,0:T(8,128)(2,1)S(1)}, bf16[80,1408]{1,0:T(8,128)(2,1)S(1)}, u32[]{:S(2)}, u32[]{:S(2)}) collective-permute-start(bf16[80,1408]{1,0:T(8,128)(2,1)S(1)} %get-tuple-element.14), channel_id=1, source_target_pairs={{64,0},{128,64},{192,128},{0,192},{65,1},{129,65},{193,129},{1,193... | collective-permute-start | bytes 675848 | tf_op jit(solution)/shard_map/ppermute | solution.py:53
  27.6 1.0 collective-permute-start.1
  28.5 2.3 %collective-permute-start.2 = (bf16[80,1408]{1,0:T(8,128)(2,1)S(1)}, bf16[80,1408]{1,0:T(8,128)(2,1)S(1)}, u32[]{:S(2)}, u32[]{:S(2)}) collective-permute-start(bf16[80,1408]{1,0:T(8,128)(2,1)S(1)} %get-tuple-element.14), channel_id=1, source_target_pairs={{192,0},{0,64},{64,128},{128,192},{193,1},{1,65},{65,129},{129,193... | collective-permute-start | bytes 675848 | tf_op jit(solution)/shard_map/ppermute | solution.py:53
  30.8 5.8 %collective-permute-done.refs_0_ = bf16[80,1408]{1,0:T(8,128)(2,1)S(1)} collective-permute-done((bf16[80,1408]{1,0:T(8,128)(2,1)S(1)}, bf16[80,1408]{1,0:T(8,128)(2,1)S(1)}, u32[]{:S(2)}, u32[]{:S(2)}) %collective-permute-start) | collective-permute-done | bytes 225312 | tf_op jit(solution)/shard_map/ppermute | solution.py:53
  36.6 5.6 %collective-permute-done.1.refs_1_ = bf16[80,1408]{1,0:T(8,128)(2,1)S(1)} collective-permute-done((bf16[80,1408]{1,0:T(8,128)(2,1)S(1)}, bf16[80,1408]{1,0:T(8,128)(2,1)S(1)}, u32[]{:S(2)}, u32[]{:S(2)}) %collective-permute-start.1) | collective-permute-done | bytes 225312 | tf_op jit(solution)/shard_map/ppermute | solution.py:53
  42.2 0.7 copy-done.14
  42.9 1.6 collective-permute-done.2.refs_2_
  44.5 0.7 copy-done.16
  45.2 6.3 %all-to-all-done.refs_3_.refs_9_ = bf16[4,256,1280]{2,1,0:T(8,128)(2,1)S(1)} async-done(((bf16[4,256,1280]{2,1,0:T(8,128)(2,1)}), bf16[4,256,1280]{2,1,0:T(8,128)(2,1)S(1)}, u32[]{:S(2)}, u32[]{:S(2)}) %all-to-all-start) | async-done | bytes 2621472 | tf_op jit(solution)/shard_map/all_to_all | solution.py:295
  51.5 0.9 copy-done.15
  52.4 0.9 copy-done.17
  53.4 3.0 %collective-permute-start.6 = (bf16[4,256,1280]{2,1,0:T(8,128)(2,1)S(1)}, bf16[4,256,1280]{2,1,0:T(8,128)(2,1)}, u32[]{:S(2)}, u32[]{:S(2)}) collective-permute-start(bf16[4,256,1280]{2,1,0:T(8,128)(2,1)S(1)} %all-to-all-done.refs_3_.refs_9_), channel_id=1, source_target_pairs={{2,0},{0,2},{3,1},{1,3},{6,4},{4,6},{7,5},{5,7},{10,8},{8,10},{11,... | collective-permute-start | bytes 7864328 | tf_op jit(solution)/shard_map/ppermute | solution.py:53
  56.5 2.8 %collective-permute-start.3 = (bf16[240,1408]{1,0:T(8,128)(2,1)S(1)}, bf16[240,1408]{1,0:T(8,128)(2,1)}, u32[]{:S(2)}, u32[]{:S(2)}) collective-permute-start(bf16[240,1408]{1,0:T(8,128)(2,1)S(1)} %shard_map.167.refs_5_), channel_id=1, source_target_pairs={{4,0},{8,4},{12,8},{0,12},{5,1},{9,5},{13,9},{1,13},{6,2},{10,6},{... | collective-permute-start | bytes 2027528 | tf_op jit(solution)/shard_map/ppermute | solution.py:53
  59.6 0.7 collective-permute-start.5
  60.5 27.6 %collective-permute-done.3.refs_6_ = bf16[240,1408]{1,0:T(8,128)(2,1)} collective-permute-done((bf16[240,1408]{1,0:T(8,128)(2,1)S(1)}, bf16[240,1408]{1,0:T(8,128)(2,1)}, u32[]{:S(2)}, u32[]{:S(2)}) %collective-permute-start.3) | collective-permute-done | bytes 675872 | tf_op jit(solution)/shard_map/ppermute | solution.py:53
  88.1 4.3 %collective-permute-done.5.refs_8_ = bf16[240,1408]{1,0:T(8,128)(2,1)} collective-permute-done((bf16[240,1408]{1,0:T(8,128)(2,1)S(1)}, bf16[240,1408]{1,0:T(8,128)(2,1)}, u32[]{:S(2)}, u32[]{:S(2)}) %collective-permute-start.5) | collective-permute-done | bytes 675872 | tf_op jit(solution)/shard_map/ppermute | solution.py:53
  92.4 0.9 copy-done.20
  93.3 16.9 %shard_map.169 = (bf16[8,128,1280]{2,1,0:T(8,128)(2,1)}, f32[320,1280]{1,0:T(8,128)}, bf16[320,1280]{1,0:T(8,128)(2,1)S(1)}, bf16[320,1280]{1,0:T(8,128)(2,1)}, bf16[320,1280]{1,0:T(8,128)(2,1)}) custom-call(s32[2]{0:T(128)S(1)} %pad_add_fusion.refs_0_, s32[8]{0:T(128)S(1)} %pad_add_fusion.1.refs_1_, bf16[320,1280]{1,0:T(8,128)(2,1)} %refs_2_.2, ...), custom_call_target="tpu_custom_call" | custom-call | flops 8388608000 | bytes 16384040 | tf_op jit(solution)/shard_map/pallas_call | solution.py:36
  110.2 0.9 copy-done.18
  111.2 4.2 %all-to-all-start.1 = ((bf16[8,128,1280]{2,1,0:T(8,128)(2,1)}), bf16[8,128,1280]{2,1,0:T(8,128)(2,1)S(1)}, u32[]{:S(2)}, u32[]{:S(2)}) async-start(bf16[8,128,1280]{2,1,0:T(8,128)(2,1)} %get-tuple-element.18), calls=%async_computation.1 | async-start | bytes 5242880 | tf_op jit(solution)/shard_map/all_to_all | solution.py:343
  115.3 1.5 collective-permute-start.8
  116.8 1.2 collective-permute-start.9
  118.0 48.9 %all-to-all-done.1.refs_0_ = bf16[8,128,1280]{2,1,0:T(8,128)(2,1)S(1)} async-done(((bf16[8,128,1280]{2,1,0:T(8,128)(2,1)}), bf16[8,128,1280]{2,1,0:T(8,128)(2,1)S(1)}, u32[]{:S(2)}, u32[]{:S(2)}) %all-to-all-start.1) | async-done | bytes 2621472 | tf_op jit(solution)/shard_map/all_to_all | solution.py:343
  167.0 1.3 copy-done.8
  168.3 1.3 copy-done.9
  169.6 1.5 shard_map.170
  171.1 4.4 %all-to-all-start.2 = ((bf16[8,128,256]{2,1,0:T(8,128)(2,1)}), bf16[8,128,256]{2,1,0:T(8,128)(2,1)S(1)}, u32[]{:S(2)}, u32[]{:S(2)}) async-start(bf16[8,128,256]{2,1,0:T(8,128)(2,1)} %shard_map.170), calls=%async_computation.2 | async-start | bytes 1048576 | tf_op jit(solution)/shard_map/all_to_all | solution.py:354
  175.6 1.4 copy-done.5
  177.0 3.0 %shard_map.172 = bf16[8,40,1280]{2,1,0:T(8,128)(2,1)} custom-call(s32[1]{0:T(128)} %bitcast.9.refs_0_, f32[320,1280]{1,0:T(8,128)S(1)} %copy-done.5, bf16[320,1280]{1,0:T(8,128)(2,1)} %collective-permute-done.7.refs_2_, bf16[320,1280]{1,0:T(8,128)(2,1)} %collective-permute-done.8.refs_3_, bf16[320,1280]{1,0:T(8,128)(2,1)} %collective-permute-done.9.refs_4_), custom_call_target="tpu_custom_call" | custom-call | bytes 4915204 | tf_op jit(solution)/shard_map/pallas_call | solution.py:36
  180.0 5.0 %all-to-all-done.2.refs_4_ = bf16[8,128,256]{2,1,0:T(8,128)(2,1)S(1)} async-done(((bf16[8,128,256]{2,1,0:T(8,128)(2,1)}), bf16[8,128,256]{2,1,0:T(8,128)(2,1)S(1)}, u32[]{:S(2)}, u32[]{:S(2)}) %all-to-all-start.2) | async-done | bytes 524320 | tf_op jit(solution)/shard_map/all_to_all | solution.py:354
  185.0 6.9 %all-to-all-start.3 = ((bf16[8,40,1280]{2,1,0:T(8,128)(2,1)}), bf16[8,40,1280]{2,1,0:T(8,128)(2,1)S(1)}, u32[]{:S(2)}, u32[]{:S(2)}) async-start(bf16[8,40,1280]{2,1,0:T(8,128)(2,1)} %shard_map.172), calls=%async_computation.3 | async-start | bytes 1638400 | tf_op jit(solution)/shard_map/all_to_all | solution.py:384
  192.2 3.4 %copy-done.2 = bf16[8192,512]{1,0:T(8,128)(2,1)S(1)} copy-done((bf16[8192,512]{1,0:T(8,128)(2,1)S(1)}, bf16[8192,512]{1,0:T(8,128)(2,1)}, u32[]{:S(2)}) %copy-start.2) | copy-done | bytes 8388632
  195.6 2.2 copy-done.3
  197.8 4.1 %shard_map.168.refs_3_ = bf16[256,512]{1,0:T(8,128)(2,1)S(1)} custom-call(bf16[256,8192]{1,0:T(8,128)(2,1)S(1)} %bitcast.14, bf16[8192,512]{1,0:T(8,128)(2,1)S(1)} %copy-done.2), custom_call_target="tpu_custom_call" | custom-call | flops 2147483648 | bytes 12582912 | tf_op jit(solution)/shard_map/pallas_call | solution.py:359
  202.0 2.8 %shard_map.171.refs_1_ = bf16[2,128,512]{2,1,0:T(8,128)(2,1)} custom-call(s32[8]{0:T(128)S(1)} %dynamic-slice_reduce_fusion.refs_0_, s32[2,8]{1,0:T(2,128)S(1)} %copy-done.21, s32[2]{0:T(128)S(1)} %copy-done.22, bf16[256,512]{1,0:T(8,128)(2,1)S(1)} %shard_map.168.refs_3_, bf16[8,128,256]{2,1,0:T(8,128)(2,1)S(1)} %all-to-all-done.2.refs_4_), custom_call_target="tpu_custom_call" | custom-call | flops 536870912 | bytes 1048680 | tf_op jit(solution)/shard_map/pallas_call | solution.py:36
  204.8 11.4 %all-to-all-done.3.refs_0_ = bf16[8,40,1280]{2,1,0:T(8,128)(2,1)S(1)} async-done(((bf16[8,40,1280]{2,1,0:T(8,128)(2,1)}), bf16[8,40,1280]{2,1,0:T(8,128)(2,1)S(1)}, u32[]{:S(2)}, u32[]{:S(2)}) %all-to-all-start.3) | async-done | bytes 819232 | tf_op jit(solution)/shard_map/all_to_all | solution.py:384
  216.2 0.9 copy-done.13
  217.1 0.8 shard_map.173
  (48 shorter events, 1.7 us)
Async XLA Ops:
  7.2 53.1 %copy-start = (s32[16,8,2]{0,2,1:T(2,128)S(1)}, s32[16,8,2]{0,2,1:T(2,128)}, u32[]{:S(2)}) copy-start(s32[16,8,2]{0,2,1:T(2,128)} %param.26) | copy-start | bytes 3076
  9.3 1.0 copy-start.6
  10.2 1.1 copy-start.10
  11.4 1.1 copy-start.11
  12.5 1.0 copy-start.12
  14.6 1.5 copy-start.4
  16.1 0.6 copy-start.19
  16.7 34.8 %all-to-all-start = ((bf16[4,256,1280]{2,1,0:T(8,128)(2,1)}), bf16[4,256,1280]{2,1,0:T(8,128)(2,1)S(1)}, u32[]{:S(2)}, u32[]{:S(2)}) async-start(bf16[4,256,1280]{2,1,0:T(8,128)(2,1)} %copy-done.4), calls=%async_computation | async-start | bytes 5242880 | tf_op jit(solution)/shard_map/all_to_all | solution.py:295
  21.5 170.7 %all-gather.2.cloned.1.call-start = ((), (), s32[]{:S(2)}) async-start(), calls=%async_computation.4 | async-start | bytes 8912896 | tf_op jit(solution)/shard_map/all_gather | solution.py:298
  21.5 15.1 %collective-permute-start = (bf16[80,1408]{1,0:T(8,128)(2,1)S(1)}, bf16[80,1408]{1,0:T(8,128)(2,1)S(1)}, u32[]{:S(2)}, u32[]{:S(2)}) collective-permute-start(bf16[80,1408]{1,0:T(8,128)(2,1)S(1)} %get-tuple-element.14), channel_id=1, source_target_pairs={{64,0},{128,64},{192,128},{0,192},{65,1},{129,65},{193,129},{1,193... | collective-permute-start | bytes 675848 | tf_op jit(solution)/shard_map/ppermute | solution.py:53
  27.6 14.6 %collective-permute-start.1 = (bf16[80,1408]{1,0:T(8,128)(2,1)S(1)}, bf16[80,1408]{1,0:T(8,128)(2,1)S(1)}, u32[]{:S(2)}, u32[]{:S(2)}) collective-permute-start(bf16[80,1408]{1,0:T(8,128)(2,1)S(1)} %get-tuple-element.14), channel_id=1, source_target_pairs={{128,0},{192,64},{0,128},{64,192},{129,1},{193,65},{1,129},{65,193... | collective-permute-start | bytes 675848 | tf_op jit(solution)/shard_map/ppermute | solution.py:53
  28.5 15.9 %collective-permute-start.2 = (bf16[80,1408]{1,0:T(8,128)(2,1)S(1)}, bf16[80,1408]{1,0:T(8,128)(2,1)S(1)}, u32[]{:S(2)}, u32[]{:S(2)}) collective-permute-start(bf16[80,1408]{1,0:T(8,128)(2,1)S(1)} %get-tuple-element.14), channel_id=1, source_target_pairs={{192,0},{0,64},{64,128},{128,192},{193,1},{1,65},{65,129},{129,193... | collective-permute-start | bytes 675848 | tf_op jit(solution)/shard_map/ppermute | solution.py:53
  42.2 0.7 copy-start.14
  44.5 0.7 copy-start.16
  51.5 0.9 copy-start.15
  52.4 0.9 copy-start.17
  53.4 39.1 %copy-start.1 = (bf16[4,256,1280]{2,1,0:T(8,128)(2,1)}, bf16[4,256,1280]{2,1,0:T(8,128)(2,1)S(1)}, u32[]{:S(2)}) copy-start(bf16[4,256,1280]{2,1,0:T(8,128)(2,1)S(1)} %all-to-all-done.refs_3_.refs_9_) | copy-start | bytes 7864324
  53.4 39.0 %collective-permute-start.6 = (bf16[4,256,1280]{2,1,0:T(8,128)(2,1)S(1)}, bf16[4,256,1280]{2,1,0:T(8,128)(2,1)}, u32[]{:S(2)}, u32[]{:S(2)}) collective-permute-start(bf16[4,256,1280]{2,1,0:T(8,128)(2,1)S(1)} %all-to-all-done.refs_3_.refs_9_), channel_id=1, source_target_pairs={{2,0},{0,2},{3,1},{1,3},{6,4},{4,6},{7,5},{5,7},{10,8},{8,10},{11,... | collective-permute-start | bytes 7864328 | tf_op jit(solution)/shard_map/ppermute | solution.py:53
  56.5 31.6 %collective-permute-start.3 = (bf16[240,1408]{1,0:T(8,128)(2,1)S(1)}, bf16[240,1408]{1,0:T(8,128)(2,1)}, u32[]{:S(2)}, u32[]{:S(2)}) collective-permute-start(bf16[240,1408]{1,0:T(8,128)(2,1)S(1)} %shard_map.167.refs_5_), channel_id=1, source_target_pairs={{4,0},{8,4},{12,8},{0,12},{5,1},{9,5},{13,9},{1,13},{6,2},{10,6},{... | collective-permute-start | bytes 2027528 | tf_op jit(solution)/shard_map/ppermute | solution.py:53
  59.2 28.9 %collective-permute-start.4 = (bf16[240,1408]{1,0:T(8,128)(2,1)S(1)}, bf16[240,1408]{1,0:T(8,128)(2,1)}, u32[]{:S(2)}, u32[]{:S(2)}) collective-permute-start(bf16[240,1408]{1,0:T(8,128)(2,1)S(1)} %shard_map.167.refs_5_), channel_id=1, source_target_pairs={{8,0},{12,4},{0,8},{4,12},{9,1},{13,5},{1,9},{5,13},{10,2},{14,6},... | collective-permute-start | bytes 2027528 | tf_op jit(solution)/shard_map/ppermute | solution.py:53
  59.6 32.8 %collective-permute-start.5 = (bf16[240,1408]{1,0:T(8,128)(2,1)S(1)}, bf16[240,1408]{1,0:T(8,128)(2,1)}, u32[]{:S(2)}, u32[]{:S(2)}) collective-permute-start(bf16[240,1408]{1,0:T(8,128)(2,1)S(1)} %shard_map.167.refs_5_), channel_id=1, source_target_pairs={{12,0},{0,4},{4,8},{8,12},{13,1},{1,5},{5,9},{9,13},{14,2},{2,6},{... | collective-permute-start | bytes 2027528 | tf_op jit(solution)/shard_map/ppermute | solution.py:53
  92.4 0.9 copy-start.20
  110.2 0.9 copy-start.18
  111.2 6.9 %copy-start.23 = (f32[1280]{0:T(1024)S(1)}, f32[1280]{0:T(1024)}, u32[]{:S(2)}) copy-start(f32[1280]{0:T(1024)} %param.21) | copy-start | bytes 15364
  111.2 55.8 %copy-start.7 = (bf16[1,4,32,1280]{3,2,1,0:T(8,128)(2,1)S(1)}, bf16[1,4,32,1280]{3,2,1,0:T(8,128)(2,1)}, u32[]{:S(2)}) copy-start(bf16[1,4,32,1280]{3,2,1,0:T(8,128)(2,1)} %param.15) | copy-start | bytes 983044
  111.2 55.8 %all-to-all-start.1 = ((bf16[8,128,1280]{2,1,0:T(8,128)(2,1)}), bf16[8,128,1280]{2,1,0:T(8,128)(2,1)S(1)}, u32[]{:S(2)}, u32[]{:S(2)}) async-start(bf16[8,128,1280]{2,1,0:T(8,128)(2,1)} %get-tuple-element.18), calls=%async_computation.1 | async-start | bytes 5242880 | tf_op jit(solution)/shard_map/all_to_all | solution.py:343
  115.3 60.2 %collective-permute-start.7 = (bf16[320,1280]{1,0:T(8,128)(2,1)}, bf16[320,1280]{1,0:T(8,128)(2,1)}, u32[]{:S(2)}, u32[]{:S(2)}) collective-permute-start(bf16[320,1280]{1,0:T(8,128)(2,1)} %copy-done.18), channel_id=1, source_target_pairs={{0,4},{4,8},{8,12},{12,0},{1,5},{5,9},{9,13},{13,1},{2,6},{6,10},{... | collective-permute-start | bytes 2457608 | tf_op jit(solution)/shard_map/ppermute | solution.py:58
  115.3 60.2 %collective-permute-start.8 = (bf16[320,1280]{1,0:T(8,128)(2,1)}, bf16[320,1280]{1,0:T(8,128)(2,1)}, u32[]{:S(2)}, u32[]{:S(2)}) collective-permute-start(bf16[320,1280]{1,0:T(8,128)(2,1)} %get-tuple-element.21), channel_id=1, source_target_pairs={{0,8},{4,12},{8,0},{12,4},{1,9},{5,13},{9,1},{13,5},{2,10},{6,14},... | collective-permute-start | bytes 2457608 | tf_op jit(solution)/shard_map/ppermute | solution.py:58
  116.8 58.7 %collective-permute-start.9 = (bf16[320,1280]{1,0:T(8,128)(2,1)}, bf16[320,1280]{1,0:T(8,128)(2,1)}, u32[]{:S(2)}, u32[]{:S(2)}) collective-permute-start(bf16[320,1280]{1,0:T(8,128)(2,1)} %get-tuple-element.22), channel_id=1, source_target_pairs={{0,12},{4,0},{8,4},{12,8},{1,13},{5,1},{9,5},{13,9},{2,14},{6,2},{... | collective-permute-start | bytes 2457608 | tf_op jit(solution)/shard_map/ppermute | solution.py:58
  167.0 1.3 copy-start.8
  168.3 1.3 copy-start.9
  171.1 13.9 %all-to-all-start.2 = ((bf16[8,128,256]{2,1,0:T(8,128)(2,1)}), bf16[8,128,256]{2,1,0:T(8,128)(2,1)S(1)}, u32[]{:S(2)}, u32[]{:S(2)}) async-start(bf16[8,128,256]{2,1,0:T(8,128)(2,1)} %shard_map.170), calls=%async_computation.2 | async-start | bytes 1048576 | tf_op jit(solution)/shard_map/all_to_all | solution.py:354
  175.6 1.4 copy-start.5
  185.0 31.2 %all-to-all-start.3 = ((bf16[8,40,1280]{2,1,0:T(8,128)(2,1)}), bf16[8,40,1280]{2,1,0:T(8,128)(2,1)S(1)}, u32[]{:S(2)}, u32[]{:S(2)}) async-start(bf16[8,40,1280]{2,1,0:T(8,128)(2,1)} %shard_map.172), calls=%async_computation.3 | async-start | bytes 1638400 | tf_op jit(solution)/shard_map/all_to_all | solution.py:384
  192.2 3.4 %copy-start.2 = (bf16[8192,512]{1,0:T(8,128)(2,1)S(1)}, bf16[8192,512]{1,0:T(8,128)(2,1)}, u32[]{:S(2)}) copy-start(bf16[8192,512]{1,0:T(8,128)(2,1)} %all-gather.2.cloned.1.call-done.weight) | copy-start | bytes 25165828
  195.6 2.2 copy-start.3
  197.8 4.2 %copy-start.21 = (s32[2,8]{1,0:T(2,128)S(1)}, s32[2,8]{1,0:T(2,128)}, u32[]{:S(2)}) copy-start(s32[2,8]{1,0:T(2,128)} %refs_1_.1) | copy-start | bytes 196
  197.8 4.2 %copy-start.22 = (s32[2]{0:T(128)S(1)}, s32[2]{0:T(128)}, u32[]{:S(2)}) copy-start(s32[2]{0:T(128)} %refs_2_.3) | copy-start | bytes 28
  216.2 1.0 copy-start.13
Sparse Core Ops, SparseCore 0:
  53.6 110.9 all-gather.1
